TPU v7x, 128 devices: a whole 4x4x4 slice. The times are simulated.
128 devices in a mesh: dp: 8 (over z_hi, x), shard: 16 (over y, z_lo, core).
Axes of the slice: x: 4, y: 4, z: 4 (z_hi: 2, z_lo: 2; z = z_hi * 2 + z_lo), core: 2. Of those that a mesh axis runs over, the one named last changes fastest.
Arguments:
- gradients: bfloat16 [8, 8, 1572864], P('dp', None, 'shard'), may hold values from -32 to 32
- master: float32 [12582912], P(('dp', 'shard'))
- moment: float32 [12582912], P(('dp', 'shard')), may hold values from -1.5 to 1.5
- second: float32 [12582912], P(('dp', 'shard')), may hold values from 0.05 to 2
- segment_ids: int32 [98304], P(('dp', 'shard')), may hold values from 0 to 63, never falling along the last dimension, each value on 1 to 3072 neighbouring positions
Outputs:
- weights: bfloat16 [8, 1572864], P(None, 'shard')
- new_master: float32 [12582912], P(('dp', 'shard'))
- new_moment: float32 [12582912], P(('dp', 'shard'))
- new_second: float32 [12582912], P(('dp', 'shard'))
Inputs may be any that keep to these rules, and one draw needn't show every extreme that they name: segment_ids never falls along the flat vector; each tensor has 1 to 3072 blocks and one has exactly 3072.
All inputs are finite; a program needn't handle non-finite values.
Results may differ from a plain program's by a relative error of at most 0.0004.
Values may be sent and summed in bfloat16 or wider, within the bound.
A program may use at most 64 MiB of HBM per device.

v0:
```python
import jax
import jax.numpy as jnp
from jax import lax
from jax.sharding import Mesh
from jax.sharding import PartitionSpec as P

DP = ("dp_0", "dp_1")
SHARD = ("shard_0", "shard_1", "shard_2")
DP_SHARD = ("dp_0", "dp_1", "shard_0", "shard_1", "shard_2")
first_fix = 1.0 - 0.9**20
second_fix = 1.0 - 0.999**20
learn_rate = 0.2
decay_rate = 0.01
tiny_eps = 1e-06


def one_axis_at_a_time(array, axes):
    for axis in axes:
        array = lax.psum(array, axis)
    return array


def joined_along(pieces, dim):
    lengths = list(pieces.shape[1:])
    lengths[dim] *= pieces.shape[0]
    return jnp.moveaxis(pieces, 0, dim).reshape(lengths)


def copy_for_each(array, axis):
    copies = jnp.broadcast_to(array, (lax.axis_size(axis), *array.shape))
    return lax.all_to_all(copies, axis, split_axis=0, concat_axis=0, tiled=True)


def gather_directly(array, axis, dim):
    return joined_along(copy_for_each(array, axis), dim)


def moments(summed, master_part, moment_part, second_part, replicas):
    grad = summed / replicas
    next_moment = 0.9 * moment_part + 0.1 * grad
    next_second = 0.999 * second_part + 0.001 * grad * grad
    update_dir = (
        next_moment / first_fix / (jnp.sqrt(next_second / second_fix) + tiny_eps)
        + decay_rate * master_part
    )
    return (next_moment, next_second, update_dir)


def tensor_sums(values, onehot):
    block_sq = jnp.sum((values * values).reshape(onehot.shape[0], -1), axis=1)
    return jnp.dot(block_sq, onehot, precision=lax.Precision.HIGHEST)


def on_device(gradients, master, moment, second, segment_ids):
    replicas = lax.axis_size(DP)
    tensors = lax.axis_size(DP) * lax.axis_size(SHARD) // 2
    blocks = segment_ids.shape[0]
    onehot = (segment_ids[:, None] == jnp.arange(tensors, dtype=jnp.int32)[None, :]).astype(
        jnp.float32
    )
    received = lax.all_to_all(gradients[0], DP, split_axis=0, concat_axis=0, tiled=True)
    summed = jnp.sum(received.astype(jnp.float32), axis=0)
    new_moment, new_second, update_dir = moments(summed, master, moment, second, replicas)
    weight_sq, update_sq = (
        one_axis_at_a_time(tensor_sums(master, onehot), DP_SHARD),
        one_axis_at_a_time(tensor_sums(update_dir, onehot), DP_SHARD),
    )
    trust = jnp.sqrt(weight_sq) / (jnp.sqrt(update_sq) + tiny_eps)
    block_trust = jnp.dot(onehot, trust, precision=lax.Precision.HIGHEST)
    new_master = master - learn_rate * (
        update_dir.reshape(blocks, -1) * block_trust[:, None]
    ).reshape(-1)
    rounded = new_master.astype(jnp.bfloat16)[None, :]
    weights = gather_directly(rounded, DP, 0)
    return (weights, new_master, new_moment, new_second)


def solution(mesh):
    torus = Mesh(
        mesh.devices.reshape(2, 4, 4, 2, 2), ("dp_0", "dp_1", "shard_0", "shard_1", "shard_2")
    )
    return jax.shard_map(
        on_device,
        mesh=torus,
        in_specs=(P(DP, None, SHARD), P(DP_SHARD), P(DP_SHARD), P(DP_SHARD), P(DP_SHARD)),
        out_specs=(P(None, SHARD), P(DP_SHARD), P(DP_SHARD), P(DP_SHARD)),
        check_vma=False,
    )
```

profile of v0, /device:TPU:1, one launch (start us, length us, event | category | flops | bytes accessed | tf_op | source)
XLA Modules:
  0.0 132.3 jit_solution(17424147377295384235)
XLA Ops:
  0.6 0.5 broadcast.10
  1.2 3.2 %reduce.3 = bf16[8,98304]{1,0:T(8,128)(2,1)S(1)} reduce(bf16[8,1,98304]{2,0,1:T(8,128)(2,1)} %bitcast.24, bf16[]{:T(256)} %broadcast.10), dimensions={1}, to_apply=%copy.10.reduce_sub_computation | reduce | bytes 3145730 | tf_op jit(solution)/shard_map/all_to_all | solution.py:61
  4.4 1.4 %reshape.36 = bf16[8,2,49152]{2,1,0:T(2,128)(2,1)S(1)} reshape(bf16[8,98304]{1,0:T(8,128)(2,1)S(1)} %reduce.3) | data formatting | bytes 3145728
  5.8 30.0 %all_to_all.14 = bf16[8,2,49152]{2,1,0:T(2,128)(2,1)} all-to-all(bf16[8,2,49152]{2,1,0:T(2,128)(2,1)S(1)} %reshape.36), channel_id=1, replica_groups=mesh['dp_0'=2,'dp_1'=4,'shard_0'=4,'shard_1'=2,'shard_2'=2] {'dp_0','dp_1'}, dimensions={0} | all-to-all | bytes 3145728 | tf_op jit(solution)/shard_map/all_to_all | solution.py:61
  35.8 4.7 %reshape.37 = bf16[8,1,98304]{2,1,0:T(2,128)(2,1)S(1)} reshape(bf16[8,2,49152]{2,1,0:T(2,128)(2,1)} %all_to_all.14) | data formatting | bytes 3145728
  40.5 4.1 %convert_reduce_fusion = f32[98304]{0:T(1024)S(1)} fusion(bf16[8,1,98304]{2,1,0:T(2,128)(2,1)S(1)} %reshape.37), kind=kLoop, calls=%fused_computation | loop fusion | flops 1474560 | bytes 1966080 | tf_op jit(solution)/shard_map/reduce_sum | solution.py:62
  44.7 0.4 bitcast_reduce_fusion.1
  45.2 0.0 copy-start.1
  45.2 0.2 copy-done.5
  45.4 0.3 convolution_bitcast_fusion.1
  45.7 0.3 convolution_bitcast_fusion
  46.0 5.3 %all-reduce.4 = (f32[64]{0:T(128)S(1)}, f32[64]{0:T(128)S(1)}) all-reduce(f32[64]{0:T(128)S(1)} %convolution_bitcast_fusion, f32[64]{0:T(128)S(1)} %convolution_bitcast_fusion.1), channel_id=1, replica_groups=mesh['dp_0'=2,'dp_1'=4,'shard_0'=4,'shard_1'=2,'shard_2'=2] {'dp_0'}, use_global_device_ids=true, to_apply=%region_8.0 | all-reduce | flops 128 | bytes 1024 | tf_op jit(solution)/shard_map/psum | solution.py:19
  51.3 6.7 %all-reduce.1 = (f32[64]{0:T(128)S(1)}, f32[64]{0:T(128)S(1)}) all-reduce(f32[64]{0:T(128)S(1)} %get-tuple-element.14, f32[64]{0:T(128)S(1)} %get-tuple-element.15), channel_id=1, replica_groups=mesh['dp_0'=2,'dp_1'=4,'shard_0'=4,'shard_1'=2,'shard_2'=2] {'dp_1'}, use_global_device_ids=true, to_apply=%region_9.0 | all-reduce | flops 128 | bytes 1024 | tf_op jit(solution)/shard_map/psum | solution.py:19
  58.0 8.7 %all-reduce = (f32[64]{0:T(128)S(1)}, f32[64]{0:T(128)S(1)}) all-reduce(f32[64]{0:T(128)S(1)} %get-tuple-element.8, f32[64]{0:T(128)S(1)} %get-tuple-element.9), channel_id=1, replica_groups=mesh['dp_0'=2,'dp_1'=4,'shard_0'=4,'shard_1'=2,'shard_2'=2] {'shard_0'}, use_global_device_ids=true, to_apply=%region_10.0 | all-reduce | flops 128 | bytes 1024 | tf_op jit(solution)/shard_map/psum | solution.py:19
  66.7 3.8 %all-reduce.3 = (f32[64]{0:T(128)S(1)}, f32[64]{0:T(128)S(1)}) all-reduce(f32[64]{0:T(128)S(1)} %get-tuple-element.6, f32[64]{0:T(128)S(1)} %get-tuple-element.7), channel_id=1, replica_groups=mesh['dp_0'=2,'dp_1'=4,'shard_0'=4,'shard_1'=2,'shard_2'=2] {'shard_1'}, use_global_device_ids=true, to_apply=%region_11.0 | all-reduce | flops 128 | bytes 1024 | tf_op jit(solution)/shard_map/psum | solution.py:19
  70.5 10.7 %all-reduce.2 = (f32[64]{0:T(128)S(1)}, f32[64]{0:T(128)S(1)}) all-reduce(f32[64]{0:T(128)S(1)} %get-tuple-element.12, f32[64]{0:T(128)S(1)} %get-tuple-element.13), channel_id=1, replica_groups=mesh['dp_0'=2,'dp_1'=4,'shard_0'=4,'shard_1'=2,'shard_2'=2] {'shard_2'}, use_global_device_ids=true, to_apply=%region_12.0 | all-reduce | flops 128 | bytes 1024 | tf_op jit(solution)/shard_map/psum | solution.py:19
  81.2 0.4 convolution_reduce_fusion
  81.7 1.0 fusion.10
  82.7 1.6 %broadcast_in_dim.2 = bf16[8,1,98304]{2,1,0:T(2,128)(2,1)S(1)} broadcast(bf16[98304]{0:T(1024)(128)(2,1)S(1)} %get-tuple-element.16), dimensions={2} | broadcast | bytes 1769472 | tf_op jit(solution)/shard_map/broadcast_in_dim | solution.py:30
  84.3 11.6 %reduce.4 = bf16[8,98304]{1,0:T(8,128)(2,1)} reduce(bf16[8,1,98304]{2,1,0:T(2,128)(2,1)S(1)} %broadcast_in_dim.2, bf16[]{:T(256)} %broadcast.10), dimensions={1}, to_apply=%broadcast_in_dim.2.reduce_sub_computation | reduce | bytes 3145730 | tf_op jit(solution)/shard_map/broadcast_in_dim | solution.py:30
  95.8 2.8 %reshape.38 = bf16[8,2,49152]{2,1,0:T(2,128)(2,1)S(1)} reshape(bf16[8,98304]{1,0:T(8,128)(2,1)} %reduce.4) | data formatting | bytes 3145728
  98.6 26.1 %all_to_all.15 = bf16[8,2,49152]{2,1,0:T(2,128)(2,1)} all-to-all(bf16[8,2,49152]{2,1,0:T(2,128)(2,1)S(1)} %reshape.38), channel_id=1, replica_groups=mesh['dp_0'=2,'dp_1'=4,'shard_0'=4,'shard_1'=2,'shard_2'=2] {'dp_0','dp_1'}, dimensions={0} | all-to-all | bytes 3145728 | tf_op jit(solution)/shard_map/all_to_all | solution.py:31
  124.7 4.7 %reshape.39 = bf16[8,1,98304]{2,1,0:T(2,128)(2,1)S(1)} reshape(bf16[8,2,49152]{2,1,0:T(2,128)(2,1)} %all_to_all.15) | data formatting | bytes 3145728
  129.4 2.9 %copy.13 = bf16[8,1,98304]{2,0,1:T(8,128)(2,1)} copy(bf16[8,1,98304]{2,1,0:T(2,128)(2,1)S(1)} %reshape.39) | data formatting | bytes 3145728
  (12 shorter events, 0.0 us)
Async XLA Ops:
  40.5 4.2 %copy-start = (f32[98304]{0:T(1024)S(1)}, f32[98304]{0:T(1024)}, u32[]{:S(2)}) copy-start(f32[98304]{0:T(1024)} %param.6) | copy-start | bytes 1179652
  40.5 4.2 %copy-start.3 = (f32[98304]{0:T(1024)S(1)}, f32[98304]{0:T(1024)}, u32[]{:S(2)}) copy-start(f32[98304]{0:T(1024)} %param.7) | copy-start | bytes 1179652
  40.5 4.2 %copy-start.4 = (f32[98304]{0:T(1024)S(1)}, f32[98304]{0:T(1024)}, u32[]{:S(2)}) copy-start(f32[98304]{0:T(1024)} %param.8) | copy-start | bytes 1179652
  44.7 0.7 copy-start.5
  45.2 37.5 %copy-start.1 = (f32[98304]{0:T(1024)}, f32[98304]{0:T(1024)S(1)}, u32[]{:S(2)}) copy-start(f32[98304]{0:T(1024)S(1)} %get-tuple-element.18) | copy-start | bytes 1179652
  45.2 37.5 %copy-start.2 = (f32[98304]{0:T(1024)}, f32[98304]{0:T(1024)S(1)}, u32[]{:S(2)}) copy-start(f32[98304]{0:T(1024)S(1)} %get-tuple-element.19) | copy-start | bytes 1179652
where the time goes:
time: 133 us; the launch traced here: 132 us
  blocking collectives  91.3 us (69%)
  other arithmetic  20.4 us (15%)
  local copies, waits for them, and re-layouts  18.7 us (14%)
    psum x5, blocking collectives, one_axis_at_a_time(): array = lax.psum(array, axis)  35.2 us
    all_to_all x1, blocking collectives, on_device(): lax.all_to_all(gradients[0], DP, split_axis=0, concat_axis=0, tiled=True)  30 us
    all_to_all x1, blocking collectives, copy_for_each(): return lax.all_to_all(copies, axis, split_axis=0, concat_axis=0, tiled=True)  26.1 us
    unnamed x17, local copies, waits for them, and re-layouts  16.6 us
    broadcast_in_dim x1, other arithmetic, copy_for_each(): copies = jnp.broadcast_to(array, (lax.axis_size(axis), *array.shape))  11.6 us
    reduce_sum x1, other arithmetic, on_device(): summed = jnp.sum(received.astype(jnp.float32), axis=0)  4.14 us
    all_to_all x1, other arithmetic, on_device(): lax.all_to_all(gradients[0], DP, split_axis=0, concat_axis=0, tiled=True)  3.23 us

commit v1 on v0

--- a/solution.py
+++ b/solution.py
@@ -16,7 +16,7 @@
 
 def one_axis_at_a_time(array, axes):
     for axis in axes:
-        array = lax.psum(array, axis)
+        array = jnp.sum(lax.all_gather(array, axis), axis=0)
     return array
 
 

time: 133 us -> 137 us (1.030)
  blocking collectives: 91.3 us -> 59.8 us
  waiting for transfers between devices: 0 us -> 16.8 us
  starting transfers between devices: 0 us -> 8.31 us
  local copies, waits for them, and re-layouts: 18.7 us -> 25.9 us
  between operations: 0.78 us -> 4.11 us
    psum x5 -> x0, blocking collectives: 35.2 us -> none  [one_axis_at_a_time(): array = lax.psum(array, axis)]
    unnamed x0 -> x5, blocking collectives: none -> 33.7 us
    all_to_all x1 -> x0, blocking collectives: 30 us -> none  [on_device(): lax.all_to_all(gradients[0], DP, split_axis=0, concat_axis=0, tiled=True)]
    all_to_all x0 -> x1, waiting for transfers between devices: none -> 16.8 us  [on_device(): lax.all_to_all(gradients[0], DP, split_axis=0, concat_axis=0, tiled=True)]
    all_to_all x0 -> x1, starting transfers between devices: none -> 8.31 us  [on_device(): lax.all_to_all(gradients[0], DP, split_axis=0, concat_axis=0, tiled=True)]
    unnamed x17 -> x52, local copies, waits for them, and re-layouts: 16.6 us -> 22.9 us
  transfers between devices with their start and end apart: 0 -> 1, of which waited for: 0 -> 1; matrix products, arithmetic and copies ran while one was open for 0% -> 2% of each run, Pallas kernels for 0% -> 0%
where the time goes in v1:
time: 137 us
  blocking collectives  59.8 us (44%)
  local copies, waits for them, and re-layouts  25.9 us (19%)
  other arithmetic  20.6 us (15%)
  waiting for transfers between devices  16.8 us (12%)
  starting transfers between devices  8.31 us (6%)
  between operations  4.11 us (3%)
    unnamed x5, blocking collectives  33.7 us
    all_to_all x1, blocking collectives, copy_for_each(): return lax.all_to_all(copies, axis, split_axis=0, concat_axis=0, tiled=True)  26.1 us
    unnamed x52, local copies, waits for them, and re-layouts  22.9 us
    all_to_all x1, waiting for transfers between devices, on_device(): lax.all_to_all(gradients[0], DP, split_axis=0, concat_axis=0, tiled=True)  16.8 us
    broadcast_in_dim x1, other arithmetic, copy_for_each(): copies = jnp.broadcast_to(array, (lax.axis_size(axis), *array.shape))  11.6 us
    all_to_all x1, starting transfers between devices, on_device(): lax.all_to_all(gradients[0], DP, split_axis=0, concat_axis=0, tiled=True)  8.31 us
    reduce_sum x1, other arithmetic, on_device(): summed = jnp.sum(received.astype(jnp.float32), axis=0)  4.14 us
    all_to_all x1, other arithmetic, on_device(): lax.all_to_all(gradients[0], DP, split_axis=0, concat_axis=0, tiled=True)  3.23 us
  transfers between devices with their start and end apart: 1, of which 1 were waited for; matrix products, arithmetic and copies ran while one was open for 2% of the time, Pallas kernels for 0%

profile of v1, /device:TPU:1, one launch (start us, length us, event | category | flops | bytes accessed | tf_op | source)
XLA Modules:
  0.0 136.6 jit_solution(15977142486316148000)
XLA Ops:
  0.6 0.5 broadcast.20
  1.2 3.2 %reduce.3 = bf16[8,98304]{1,0:T(8,128)(2,1)S(1)} reduce(bf16[8,1,98304]{2,0,1:T(8,128)(2,1)} %bitcast.29, bf16[]{:T(256)} %broadcast.20), dimensions={1}, to_apply=%copy.10.reduce_sub_computation | reduce | bytes 3145730 | tf_op jit(solution)/shard_map/all_to_all | solution.py:61
  4.4 2.5 %reshape.96 = bf16[8,2,49152]{2,1,0:T(2,128)(2,1)} reshape(bf16[8,98304]{1,0:T(8,128)(2,1)S(1)} %reduce.3) | data formatting | bytes 3145728
  6.9 8.3 %all-to-all-start = ((bf16[8,2,49152]{2,1,0:T(2,128)(2,1)}), bf16[8,2,49152]{2,1,0:T(2,128)(2,1)}, u32[]{:S(2)}, u32[]{:S(2)}) async-start(bf16[8,2,49152]{2,1,0:T(2,128)(2,1)} %reshape.96), calls=%async_computation | async-start | bytes 3145728 | tf_op jit(solution)/shard_map/all_to_all | solution.py:61
  15.2 0.6 dynamic-slice.4
  15.8 0.6 dynamic-slice.3
  17.7 0.6 dynamic-slice.2
  19.0 0.6 dynamic-slice.1
  20.2 0.6 dynamic-slice
  21.5 16.8 %all-to-all-done = bf16[8,2,49152]{2,1,0:T(2,128)(2,1)} async-done(((bf16[8,2,49152]{2,1,0:T(2,128)(2,1)}), bf16[8,2,49152]{2,1,0:T(2,128)(2,1)}, u32[]{:S(2)}, u32[]{:S(2)}) %all-to-all-start) | async-done | bytes 1572896 | tf_op jit(solution)/shard_map/all_to_all | solution.py:61
  38.3 4.7 %reshape.97 = bf16[8,1,98304]{2,1,0:T(2,128)(2,1)S(1)} reshape(bf16[8,2,49152]{2,1,0:T(2,128)(2,1)} %all-to-all-done) | data formatting | bytes 3145728
  43.0 4.1 %convert_reduce_fusion = f32[98304]{0:T(1024)S(1)} fusion(bf16[8,1,98304]{2,1,0:T(2,128)(2,1)S(1)} %reshape.97), kind=kLoop, calls=%fused_computation | loop fusion | flops 1474560 | bytes 1966080 | tf_op jit(solution)/shard_map/reduce_sum | solution.py:62
  49.0 5.3 %all-reduce.14 = (f32[128]{0:T(128)S(1)}, f32[128]{0:T(128)S(1)}) all-reduce(f32[128]{0:T(128)S(1)} %dynamic-update-slice.5, f32[128]{0:T(128)S(1)} %dynamic-update-slice), channel_id=7, replica_groups=mesh['dp_0'=2,'dp_1'=4,'shard_0'=4,'shard_1'=2,'shard_2'=2] {'dp_0'}, use_global_device_ids=true, to_apply=%add.5 | all-reduce | flops 256 | bytes 2048
  54.9 6.6 %all-reduce.11 = (f32[256]{0:T(256)S(1)}, f32[256]{0:T(256)S(1)}) all-reduce(f32[256]{0:T(256)S(1)} %dynamic-update-slice.6, f32[256]{0:T(256)S(1)} %dynamic-update-slice.1), channel_id=8, replica_groups=mesh['dp_0'=2,'dp_1'=4,'shard_0'=4,'shard_1'=2,'shard_2'=2] {'dp_1'}, use_global_device_ids=true, to_apply=%add.6 | all-reduce | flops 512 | bytes 4096
  62.2 8.7 %all-reduce.10 = (f32[256]{0:T(256)S(1)}, f32[256]{0:T(256)S(1)}) all-reduce(f32[256]{0:T(256)S(1)} %dynamic-update-slice.7, f32[256]{0:T(256)S(1)} %dynamic-update-slice.2), channel_id=9, replica_groups=mesh['dp_0'=2,'dp_1'=4,'shard_0'=4,'shard_1'=2,'shard_2'=2] {'shard_0'}, use_global_device_ids=true, to_apply=%add.7 | all-reduce | flops 512 | bytes 4096
  71.5 3.8 %all-reduce.13 = (f32[128]{0:T(128)S(1)}, f32[128]{0:T(128)S(1)}) all-reduce(f32[128]{0:T(128)S(1)} %dynamic-update-slice.8, f32[128]{0:T(128)S(1)} %dynamic-update-slice.3), channel_id=10, replica_groups=mesh['dp_0'=2,'dp_1'=4,'shard_0'=4,'shard_1'=2,'shard_2'=2] {'shard_1'}, use_global_device_ids=true, to_apply=%add.8 | all-reduce | flops 256 | bytes 2048
  76.0 9.4 %all-reduce.12 = (f32[128]{0:T(128)S(1)}, f32[128]{0:T(128)S(1)}) all-reduce(f32[128]{0:T(128)S(1)} %dynamic-update-slice.9, f32[128]{0:T(128)S(1)} %dynamic-update-slice.4), channel_id=11, replica_groups=mesh['dp_0'=2,'dp_1'=4,'shard_0'=4,'shard_1'=2,'shard_2'=2] {'shard_2'}, use_global_device_ids=true, to_apply=%add.9 | all-reduce | flops 256 | bytes 2048
  86.0 1.0 fusion.10
  87.0 1.6 %broadcast_in_dim.2 = bf16[8,1,98304]{2,1,0:T(2,128)(2,1)S(1)} broadcast(bf16[98304]{0:T(1024)(128)(2,1)S(1)} %get-tuple-element.16), dimensions={2} | broadcast | bytes 1769472 | tf_op jit(solution)/shard_map/broadcast_in_dim | solution.py:30
  88.6 11.6 %reduce.4 = bf16[8,98304]{1,0:T(8,128)(2,1)} reduce(bf16[8,1,98304]{2,1,0:T(2,128)(2,1)S(1)} %broadcast_in_dim.2, bf16[]{:T(256)} %broadcast.20), dimensions={1}, to_apply=%broadcast_in_dim.2.reduce_sub_computation | reduce | bytes 3145730 | tf_op jit(solution)/shard_map/broadcast_in_dim | solution.py:30
  100.2 2.8 %reshape.98 = bf16[8,2,49152]{2,1,0:T(2,128)(2,1)S(1)} reshape(bf16[8,98304]{1,0:T(8,128)(2,1)} %reduce.4) | data formatting | bytes 3145728
  102.9 26.1 %all_to_all.14 = bf16[8,2,49152]{2,1,0:T(2,128)(2,1)} all-to-all(bf16[8,2,49152]{2,1,0:T(2,128)(2,1)S(1)} %reshape.98), channel_id=1, replica_groups=mesh['dp_0'=2,'dp_1'=4,'shard_0'=4,'shard_1'=2,'shard_2'=2] {'dp_0','dp_1'}, dimensions={0} | all-to-all | bytes 3145728 | tf_op jit(solution)/shard_map/all_to_all | solution.py:31
  129.0 4.7 %reshape.99 = bf16[8,1,98304]{2,1,0:T(2,128)(2,1)S(1)} reshape(bf16[8,2,49152]{2,1,0:T(2,128)(2,1)} %all_to_all.14) | data formatting | bytes 3145728
  133.7 2.9 %copy.13 = bf16[8,1,98304]{2,0,1:T(8,128)(2,1)} copy(bf16[8,1,98304]{2,1,0:T(2,128)(2,1)S(1)} %reshape.99) | data formatting | bytes 3145728
  (68 shorter events, 5.0 us)
Async XLA Ops:
  6.9 8.3 %copy-start.10 = (u32[128]{0:T(128)S(1)}, u32[128]{0:T(128)}, u32[]{:S(2)}) copy-start(u32[128]{0:T(128)} %constant.51) | copy-start | bytes 1540
  6.9 8.9 %copy-start.9 = (u32[128]{0:T(128)S(1)}, u32[128]{0:T(128)}, u32[]{:S(2)}) copy-start(u32[128]{0:T(128)} %constant.46) | copy-start | bytes 1540
  6.9 10.8 %copy-start.8 = (u32[128]{0:T(128)S(1)}, u32[128]{0:T(128)}, u32[]{:S(2)}) copy-start(u32[128]{0:T(128)} %constant.41) | copy-start | bytes 1540
  6.9 12.1 %copy-start.7 = (u32[128]{0:T(128)S(1)}, u32[128]{0:T(128)}, u32[]{:S(2)}) copy-start(u32[128]{0:T(128)} %constant.36) | copy-start | bytes 1540
  6.9 13.3 %copy-start.6 = (u32[128]{0:T(128)S(1)}, u32[128]{0:T(128)}, u32[]{:S(2)}) copy-start(u32[128]{0:T(128)} %constant.31) | copy-start | bytes 1540
  6.9 31.3 %all-to-all-start = ((bf16[8,2,49152]{2,1,0:T(2,128)(2,1)}), bf16[8,2,49152]{2,1,0:T(2,128)(2,1)}, u32[]{:S(2)}, u32[]{:S(2)}) async-start(bf16[8,2,49152]{2,1,0:T(2,128)(2,1)} %reshape.96), calls=%async_computation | async-start | bytes 3145728 | tf_op jit(solution)/shard_map/all_to_all | solution.py:61
  43.0 4.2 %copy-start = (f32[98304]{0:T(1024)S(1)}, f32[98304]{0:T(1024)}, u32[]{:S(2)}) copy-start(f32[98304]{0:T(1024)} %param.6) | copy-start | bytes 1179652
  43.0 4.2 %copy-start.3 = (f32[98304]{0:T(1024)S(1)}, f32[98304]{0:T(1024)}, u32[]{:S(2)}) copy-start(f32[98304]{0:T(1024)} %param.7) | copy-start | bytes 1179652
  43.0 4.2 %copy-start.4 = (f32[98304]{0:T(1024)S(1)}, f32[98304]{0:T(1024)}, u32[]{:S(2)}) copy-start(f32[98304]{0:T(1024)} %param.8) | copy-start | bytes 1179652
  47.2 0.7 copy-start.5
  47.6 39.3 %copy-start.1 = (f32[98304]{0:T(1024)}, f32[98304]{0:T(1024)S(1)}, u32[]{:S(2)}) copy-start(f32[98304]{0:T(1024)S(1)} %get-tuple-element.18) | copy-start | bytes 1179652
  47.7 39.3 %copy-start.2 = (f32[98304]{0:T(1024)}, f32[98304]{0:T(1024)S(1)}, u32[]{:S(2)}) copy-start(f32[98304]{0:T(1024)S(1)} %get-tuple-element.19) | copy-start | bytes 1179652
